TPU v7x, 32 devices: a whole 2x2x4 slice. The times are simulated.
32 devices in a mesh: col: 4 (over y, core), row: 8 (over z, x).
Axes of the slice: x: 2, y: 2, z: 4, core: 2. Of those that a mesh axis runs over, the one named last changes fastest.
Arguments:
- tokens: bfloat16 [2048, 2880], P('row'), may hold values from -6 to 6
- moe_gain: bfloat16 [2880], replicated, may hold values from 0.5 to 1.5
- route_ids: int32 [2048, 4], P('row'), may hold values from 0 to 63, all different within a row; in each aligned block of 256 rows (0 to 255, 256 to 511, ...) at most 24 rows name the same one
- route_weight: float32 [2048, 4], P('row'), may hold values from 0.1 to 1
- w_gate: bfloat16 [64, 2880, 2880], P('row', None, 'col'), may hold values from -0.109375 to 0.109375
- w_up: bfloat16 [64, 2880, 2880], P('row', None, 'col'), may hold values from -0.109375 to 0.109375
- w_down: bfloat16 [64, 2880, 2880], P('row', 'col'), may hold values from -0.109375 to 0.109375
- next_gain: bfloat16 [2880], replicated, may hold values from 0.5 to 1.5
- next_gate: bfloat16 [2880, 128], P(None, 'col'), may hold values from -2 to 2
- next_ids: int32 [2048, 4], P('row'), may hold values from 0 to 127, all different within a row
Outputs:
- mixed: bfloat16 [2048, 2880], P('row', 'col')
- next_logprob: float32 [2048, 4], P('row')
Inputs may be any that keep to these rules, and one draw needn't show every extreme that they name: `route_ids`: among the 256 tokens of one index of row, no expert is picked more than 24 times, a bound that some block reaches; a token's picks differ. `next_ids`: A token's picks differ.
All inputs are finite; a program needn't handle non-finite values.
Results may differ from a plain program's by a relative error of at most 0.0095.
Values may be sent and summed in bfloat16 or wider, within the bound.
A program may use at most 256 MiB of HBM per device.

v0:
```python
import jax
import jax.numpy as jnp
from jax import lax
from jax.sharding import PartitionSpec as P

TOP = 4
CAP = 24


def combined_all(value, axis, join):
    pieces = jax.tree.map(lambda part: lax.all_gather(part, axis), value)
    head = jax.tree.map(lambda part: part[0], pieces)
    tail = jax.tree.map(lambda part: part[1:], pieces)
    total, _ = lax.scan(lambda total, piece: (join(total, piece), None), head, tail)
    return total


def merge_softmax(first, second):
    highest = jnp.maximum(first[0], second[0])
    total = first[1] * jnp.exp(first[0] - highest) + second[1] * jnp.exp(second[0] - highest)
    return (highest, total, first[2] + second[2])


def local(
    tokens, moe_gain, route_ids, route_weight, w_gate, w_up, w_down, next_gain, next_gate, next_ids
):
    row_count = lax.axis_size("row")
    col_count = lax.axis_size("col")
    tok_rows = tokens.shape[0]
    feature_count = tokens.shape[1]
    local_experts = w_gate.shape[0]
    expert_count = local_experts * row_count
    part_width = feature_count // col_count
    col_start = lax.axis_index("col") * part_width
    floats = tokens.astype(jnp.float32)
    inverse = lax.rsqrt(jnp.mean(floats * floats, axis=-1, keepdims=True) + 1e-05)
    normed = (floats * inverse * moe_gain.astype(jnp.float32)).astype(jnp.bfloat16)
    gated_in = (floats * inverse * next_gain.astype(jnp.float32)).astype(jnp.bfloat16)
    flat_ids = route_ids.reshape(-1)
    onehot = (flat_ids[:, None] == jnp.arange(expert_count, dtype=jnp.int32)[None, :]).astype(
        jnp.int32
    )
    slots = jnp.sum(jnp.cumsum(onehot, axis=0) * onehot, axis=1) - 1
    target = flat_ids * CAP + slots
    token_of = jnp.arange(tok_rows * TOP, dtype=jnp.int32) // TOP
    buffer = jnp.zeros((expert_count * CAP, normed.shape[1]), jnp.bfloat16)
    buffer = buffer.at[target].set(normed[token_of])
    arrived = lax.all_to_all(
        buffer.reshape(row_count, local_experts, CAP, normed.shape[1]),
        "row",
        split_axis=0,
        concat_axis=0,
        tiled=True,
    )
    logits = jnp.dot(gated_in, next_gate, preferred_element_type=jnp.float32)
    cols_local = next_gate.shape[1]
    local_index = next_ids - lax.axis_index("col") * cols_local
    owned = (
        local_index[:, :, None] == jnp.arange(cols_local, dtype=jnp.int32)[None, None, :]
    ).astype(jnp.float32)
    picked_logit = jnp.sum(owned * logits[:, None, :], axis=-1)
    local_max = jnp.max(logits, axis=-1)
    gate = jnp.einsum("sjcd,jdf->sjcf", arrived, w_gate, preferred_element_type=jnp.float32)
    upward = jnp.einsum("sjcd,jdf->sjcf", arrived, w_up, preferred_element_type=jnp.float32)
    hidden = (jax.nn.silu(gate) * upward).astype(jnp.bfloat16)
    partial_value = jnp.einsum(
        "sjcf,jfd->sjcd", hidden, w_down, preferred_element_type=jnp.float32
    ).astype(jnp.bfloat16)
    local_sum = jnp.sum(jnp.exp(logits - local_max[:, None]), axis=-1)
    highest, total, chosen = combined_all(
        (local_max, local_sum, picked_logit), "col", merge_softmax
    )
    next_logprob = chosen - highest[:, None] - jnp.log(total)[:, None]
    summed = (
        lax.psum_scatter(partial_value, "col", scatter_dimension=3, tiled=True)
        .astype(jnp.float32)
        .astype(jnp.bfloat16)
    )
    returned = lax.all_to_all(summed, "row", split_axis=0, concat_axis=0, tiled=True)
    flat_back = returned.reshape(expert_count * CAP, part_width)
    gathered = flat_back[target].astype(jnp.float32).reshape(tok_rows, TOP, part_width)
    combined = jnp.sum(gathered * route_weight[:, :, None], axis=1)
    residual = lax.dynamic_slice_in_dim(floats, col_start, part_width, 1)
    mixed = (residual + combined).astype(jnp.bfloat16)
    return (mixed, next_logprob)


def solution(mesh):
    placed = (
        P("row", None),
        P(),
        P("row", None),
        P("row", None),
        P("row", None, "col"),
        P("row", None, "col"),
        P("row", "col", None),
        P(),
        P(None, "col"),
        P("row", None),
    )
    return jax.shard_map(
        local,
        mesh=mesh,
        in_specs=placed,
        out_specs=(P("row", "col"), P("row", None)),
        check_vma=False,
    )
```

profile of v0, /device:TPU:0, one launch (start us, length us, event | category | flops | bytes accessed | tf_op | source)
XLA Modules:
  0.0 618.7 jit_solution(248528182647573483)
XLA Ops:
  7.2 0.0 copy-start
  7.2 0.0 copy-start.2
  7.2 0.0 reduce-scatter.4.cloned.1.call-start
  7.2 0.7 broadcast_multiply_fusion
  7.9 0.8 copy.56
  8.7 0.1 eq.42
  8.9 0.1 eq.38
  9.0 0.1 copy.55
  9.1 0.1 mul.88
  9.3 18.0 %reduce-window.6 = s32[64,8,128]{2,1,0:T(8,128)S(1)} reduce-window(s32[64,8,128]{2,1,0:T(8,128)S(1)} %fusion.26, s32[]{:T(128)} %copy.97), window={size=1x1x128 pad=0_0x0_0x127_0}, to_apply=%region_0.0 | reduce-window | flops 8323072 | bytes 524292 | tf_op jit(solution)/shard_map/reduce-window
  27.3 0.1 slice.46
  27.4 0.1 copy.58
  27.6 0.1 copy.59
  27.7 0.1 broadcast_add_fusion
  27.9 0.1 fusion.25
  27.9 1.8 copy.54
  29.8 0.0 copy-done.2
  29.8 0.0 copy-start.1
  29.8 0.4 multiply_reduce_fusion.1
  30.2 0.4 multiply_convert_fusion.1
  30.7 32.5 %scatter_custom_fusion = bf16[1536,2880]{1,0:T(8,128)(2,1)} fusion(s32[1024]{0:T(1024)S(1)} %bitcast.98, bf16[256,2880]{1,0:T(8,128)(2,1)S(1)} %multiply_convert_fusion.1, s32[1024]{0:T(1024)S(1)} %broadcast_clamp_fusion.1, bf16[]{:T(256)} %constant.54.clone.1), kind=kCustom, calls=%fused_computation.16 | custom fusion | bytes 8847362 | tf_op jit(solution)/shard_map/scatter | solution.py:47
  63.2 0.0 copy-done.1
  63.2 205.2 %all_to_all.10 = bf16[8,8,24,2880]{3,2,1,0:T(8,128)(2,1)} all-to-all(bf16[8,8,24,2880]{3,2,1,0:T(8,128)(2,1)} %bitcast.88), channel_id=1, replica_groups=mesh['col'=4,'row'=8] {'row'}, dimensions={0} | all-to-all | bytes 17694720 | tf_op jit(solution)/shard_map/all_to_all | solution.py:48
  268.4 18.9 %fusion.2 = f32[8,8,24,720]{3,2,1,0:T(8,128)} fusion(bf16[8,2880,720]{1,2,0:T(8,128)(2,1)} %param.17, bf16[8,8,24,2880]{3,2,1,0:T(8,128)(2,1)} %all_to_all.10), kind=kOutput, calls=%fused_computation.9 | convolution fusion | flops 6370099200 | bytes 46448640 | tf_op jit(solution)/shard_map/sjcd,jdf->sjcf/dot_general | solution.py:64
  287.3 19.8 %fusion.12 = bf16[8,8,24,720]{3,2,0,1:T(8,128)(2,1)S(1)} fusion(f32[8,8,24,720]{3,2,1,0:T(8,128)} %fusion.2, bf16[8,2880,720]{1,2,0:T(8,128)(2,1)} %param.16, bf16[8,8,24,2880]{3,2,1,0:T(8,128)(2,1)} %all_to_all.10), kind=kOutput, calls=%fused_computation.19 | convolution fusion | flops 6376734720 | bytes 48660480 | tf_op jit(solution)/shard_map/sjcd,jdf->sjcf/dot_general | solution.py:63
  307.1 16.6 %convert_bitcast_fusion = bf16[8,8,24,2880]{3,2,0,1:T(8,128)(2,1)} fusion(bf16[8,8,24,720]{3,2,0,1:T(8,128)(2,1)S(1)} %fusion.12, bf16[8,720,2880]{2,1,0:T(8,128)(2,1)} %param.18), kind=kOutput, calls=%fused_computation.13 | convolution fusion | flops 6374522880 | bytes 44236800 | tf_op jit(solution)/shard_map/sjcf,jfd->sjcd/dot_general | solution.py:66
  323.7 42.9 %copy.68 = bf16[8,8,24,2880]{2,0,1,3:T(8,128)(2,1)} copy(bf16[8,8,24,2880]{3,2,0,1:T(8,128)(2,1)} %convert_bitcast_fusion) | data formatting | bytes 17694720
  366.7 64.5 %reshape.177 = bf16[2880,1536]{1,0:T(8,128)(2,1)} reshape(bf16[2880,8,8,24]{3,2,1,0:T(8,128)(2,1)} %bitcast.85) | data formatting | bytes 17694720
  431.2 0.0 reduce-scatter.4.cloned.1.call-update
  431.2 73.1 %reduce-scatter.4.cloned.1.call-done = bf16[720,1536]{1,0:T(8,128)(2,1)} async-done(((bf16[2880,1536]{1,0:T(8,128)(2,1)}), bf16[720,1536]{1,0:T(8,128)(2,1)}) %reduce-scatter.4.cloned.1.call-update) | async-done | bytes 2211856
  504.3 21.3 %reshape.178 = bf16[720,8,8,24]{3,2,1,0:T(8,128)(2,1)} reshape(bf16[720,1536]{1,0:T(8,128)(2,1)} %reduce-scatter.4.cloned.1.call-done) | data formatting | bytes 4423680
  525.6 14.2 %copy.62 = bf16[8,8,24,720]{3,2,1,0:T(8,128)(2,1)} copy(bf16[8,8,24,720]{2,0,1,3:T(8,128)(2,1)} %bitcast.87) | data formatting | bytes 4423680 | tf_op jit(solution)/shard_map/reduce_scatter | solution.py:75
  539.9 0.0 copy-start.3
  539.9 5.6 all-to-all-start.1
  545.5 0.0 copy-start.5
  545.5 0.0 copy-start.4
  545.5 3.2 convert_element_type.42
  548.7 0.0 copy-done.3
  548.8 0.0 copy-done
  548.8 2.1 fusion.27
  550.8 5.1 all-gather.3
  555.9 5.1 all-gather.4
  561.0 0.0 copy-done.5
  561.0 5.2 all-gather.2
  566.2 0.0 copy-done.4
  566.2 0.1 copy.63
  566.4 0.2 while.14
  566.6 0.6 subtract_subtract_fusion
  567.2 32.0 %all-to-all-done.1 = bf16[8,8,24,720]{3,2,1,0:T(8,128)(2,1)S(1)} async-done(((bf16[8,8,24,720]{3,2,1,0:T(8,128)(2,1)}), bf16[8,8,24,720]{3,2,1,0:T(8,128)(2,1)S(1)}, u32[]{:S(2)}, u32[]{:S(2)}) %all-to-all-start.1) | async-done | bytes 2211872 | tf_op jit(solution)/shard_map/all_to_all | solution.py:79
  599.2 5.2 gather_fusion
  604.5 2.9 reshape.127
  607.4 2.0 multiply_reduce_fusion
  609.3 1.5 add_convert_fusion
  610.8 0.9 copy.64
  (32 shorter events, 0.3 us)
Async XLA Ops:
  7.2 541.6 %copy-start = (bf16[2880,32]{0,1:T(8,128)(2,1)S(1)}, bf16[2880,32]{0,1:T(8,128)(2,1)}, u32[]{:S(2)}) copy-start(bf16[2880,32]{0,1:T(8,128)(2,1)} %param.20) | copy-start | bytes 552964
  7.2 22.6 %copy-start.2 = (bf16[2880]{0:T(1024)(128)(2,1)S(1)}, bf16[2880]{0:T(1024)(128)(2,1)}, u32[]{:S(2)}) copy-start(bf16[2880]{0:T(1024)(128)(2,1)} %param.13) | copy-start | bytes 17284
  7.2 497.1 %reduce-scatter.4.cloned.1.call-start = ((), (), s32[]{:S(2)}) async-start(), calls=%async_computation.3 | async-start | bytes 11059200
  29.8 33.4 %copy-start.1 = (bf16[256,2880]{1,0:T(8,128)(2,1)}, bf16[256,2880]{1,0:T(8,128)(2,1)S(1)}, u32[]{:S(2)}) copy-start(bf16[256,2880]{1,0:T(8,128)(2,1)S(1)} %copy.54) | copy-start | bytes 4423684
  539.9 8.9 %copy-start.3 = (bf16[2880]{0:T(1024)(128)(2,1)S(1)}, bf16[2880]{0:T(1024)(128)(2,1)}, u32[]{:S(2)}) copy-start(bf16[2880]{0:T(1024)(128)(2,1)} %param.19) | copy-start | bytes 17284
  539.9 59.3 %all-to-all-start.1 = ((bf16[8,8,24,720]{3,2,1,0:T(8,128)(2,1)}), bf16[8,8,24,720]{3,2,1,0:T(8,128)(2,1)S(1)}, u32[]{:S(2)}, u32[]{:S(2)}) async-start(bf16[8,8,24,720]{3,2,1,0:T(8,128)(2,1)} %copy.62), calls=%async_computation.1 | async-start | bytes 4718592 | tf_op jit(solution)/shard_map/all_to_all | solution.py:79
  545.5 15.5 %copy-start.5 = (s32[256,4]{0,1:T(4,128)S(1)}, s32[256,4]{0,1:T(4,128)}, u32[]{:S(2)}) copy-start(s32[256,4]{0,1:T(4,128)} %param.21) | copy-start | bytes 12292
  545.5 20.7 %copy-start.4 = (f32[256,4]{0,1:T(4,128)S(1)}, f32[256,4]{0,1:T(4,128)}, u32[]{:S(2)}) copy-start(f32[256,4]{0,1:T(4,128)} %param.15) | copy-start | bytes 12292
Sparse Core Ops, SparseCore 0:
  431.3 72.9 reduce-scatter.3
where the time goes:
time: 630 us; the launch traced here: 619 us
  blocking collectives  220 us (35%)
  local copies, waits for them, and re-layouts  188 us (30%)
  waiting for transfers between devices  105 us (17%)
  matrix products  57.4 us (9%)
  other arithmetic  27.2 us (4%)
  between operations  14.4 us (2%)
    all_to_all x1, blocking collectives, local(): lax.all_to_all(buffer.reshape(row_count, local_experts, CAP, normed.shape...  205 us
    unnamed x21, local copies, waits for them, and re-layouts  132 us
    unnamed x2, waiting for transfers between devices  73.1 us
    scatter x1, local copies, waits for them, and re-layouts, local(): buffer = buffer.at[target].set(normed[token_of])  32.5 us
    all_to_all x1, waiting for transfers between devices, local(): lax.all_to_all(summed, 'row', split_axis=0, concat_axis=0, tiled=True)  32 us
    dot_general x1, matrix products, local(): jnp.einsum('sjcd,jdf->sjcf', arrived, w_gate, preferred_element_type=jnp....  19.8 us
    dot_general x1, matrix products, local(): jnp.einsum('sjcd,jdf->sjcf', arrived, w_up, preferred_element_type=jnp.fl...  18.9 us
    another operation x3, other arithmetic  18.2 us
  transfers between devices with their start and end apart: 2, of which 2 were waited for; matrix products, arithmetic and copies ran while one was open for 1% of the time, Pallas kernels for 0%

commit v1 on v0

v1 whole, which is shorter than its diff:
```python
import functools

import jax
import jax.numpy as jnp
from jax import lax
from jax.experimental import pallas as pl
from jax.experimental.pallas import tpu as pltpu
from jax.sharding import PartitionSpec as P

TOP = 4
CAP = 24


MESH = pl.DeviceIdType.MESH


def ring_place(row, rows):
    return row // 2 + (row % 2) * (rows - 1 - 2 * (row // 2))


def ring_row(place, rows):
    place = (place + 2 * rows) % rows
    far = place // (rows // 2)
    return (1 - far) * 2 * place + far * (2 * (rows - 1 - place) + 1)


def lanes_of(rows):
    half = rows // 2
    found = []
    for distance in range(1, half + 1):
        for way in (0, 1):
            for sub in (0, 1):
                if distance < half or way == sub:
                    found.append((len(found), 1 - 2 * way, sub, distance))
    return found


def remote(src, dst, send, recv, target):
    return pltpu.make_async_remote_copy(
        src_ref=src, dst_ref=dst, send_sem=send, recv_sem=recv, device_id=target, device_id_type=MESH
    )


def greet(rows, cols, all_cols):
    row, col = lax.axis_index("row"), lax.axis_index("col")
    barrier = pltpu.get_barrier_semaphore()
    for step in range(1, rows):
        pl.semaphore_signal(
            barrier, inc=1, device_id={"row": (row + step) % rows}, device_id_type=MESH
        )
    others = range(1, cols) if all_cols else ()
    for step in others:
        pl.semaphore_signal(
            barrier, inc=1, device_id={"col": (col + step) % cols}, device_id_type=MESH
        )
    pl.semaphore_wait(barrier, rows - 1 + len(others))


def gather_kernel(
    rows, cols, x_ref, info_ref, out_ref, all_ref, ring_s, ring_r, pair_s, pair_r, info_s, info_r, own_s
):
    row, col = lax.axis_index("row"), lax.axis_index("col")
    core = col % 2
    mate = {"col": col + 1 - 2 * core}
    place = ring_place(row, rows)
    tok = x_ref.shape[0]
    quarter = tok // 4
    greet(rows, cols, True)
    infos = []
    for step in range(1, rows):
        copy = remote(
            info_ref, all_ref.at[row], info_s.at[step - 1], info_r.at[step - 1],
            {"row": (row + step) % rows},
        )
        copy.start()
        infos.append(copy)
    own = pltpu.make_async_copy(x_ref, out_ref.at[row], own_s)

    def span(sub):
        return pl.ds(pl.multiple_of(core * 2 * quarter, quarter) + sub * quarter, quarter)

    lanes = lanes_of(rows)
    where = {(way, sub, far): index for index, way, sub, far in lanes}
    sends = {}

    def send(way, sub, far):
        index = where[way, sub, far]
        block = ring_row(place - way * (far - 1), rows)
        src = x_ref.at[span(sub)] if far == 1 else out_ref.at[block, span(sub)]
        copy = remote(
            src, out_ref.at[block, span(sub)], ring_s.at[index], ring_r.at[index],
            {"row": ring_row(place + way, rows)},
        )
        copy.start()
        sends[index] = copy

    for index, way, sub, far in lanes:
        if far == 1:
            send(way, sub, far)
    own.start()
    pairs = []
    for index, way, sub, far in lanes:
        sends[index].wait_recv()
        if (way, sub, far + 1) in where:
            send(way, sub, far + 1)
        block = ring_row(place - way * far, rows)
        piece = out_ref.at[block, span(sub)]
        copy = remote(piece, piece, pair_s.at[index], pair_r.at[index], mate)
        copy.start()
        pairs.append(copy)
    all_ref[row] = info_ref[...]
    for copy in infos:
        copy.wait()
    own.wait()
    for index, *_ in lanes:
        sends[index].wait_send()
    for copy in pairs:
        copy.wait()


def gather(x, info):
    rows, cols = lax.axis_size("row"), lax.axis_size("col")
    count = len(lanes_of(rows))
    dma = pltpu.SemaphoreType.DMA
    return pl.pallas_call(
        functools.partial(gather_kernel, rows, cols),
        out_shape=(
            jax.ShapeDtypeStruct((rows,) + x.shape, x.dtype),
            jax.ShapeDtypeStruct((rows,) + info.shape, info.dtype),
        ),
        in_specs=[pl.BlockSpec(memory_space=pltpu.VMEM)] * 2,
        out_specs=(pl.BlockSpec(memory_space=pl.ANY), pl.BlockSpec(memory_space=pltpu.VMEM)),
        scratch_shapes=[
            dma((count,)), dma((count,)), dma((count,)), dma((count,)),
            dma((rows - 1,)), dma((rows - 1,)), dma(()),
        ],
        compiler_params=pltpu.CompilerParams(collective_id=0, has_side_effects=True),
        name="gather",
    )(x, info)


def reduce_kernel(
    rows, cols, x_ref, out_ref, mate_buf, got, made, last, parts,
    pair_s, pair_r, ring_s, ring_r, col_s, col_r,
):
    row, col = lax.axis_index("row"), lax.axis_index("col")
    core = col % 2
    place = ring_place(row, rows)
    tok, dim = x_ref.shape[1:]
    quarter = tok // 4
    part = dim // cols
    strip = 16
    greet(rows, cols, True)
    lanes = lanes_of(rows)
    where = {(way, sub, far): index for index, way, sub, far in lanes}
    wanted = list(reversed(lanes)) + [(len(lanes), 1, 0, 0), (len(lanes) + 1, 1, 1, 0)]

    def start_of(owner, sub):
        return pl.multiple_of(owner * 2 * quarter, quarter) + sub * quarter

    pairs = {}
    for index, way, sub, far in wanted:
        block = ring_row(place + way * far, rows)
        copy = remote(
            x_ref.at[block, pl.ds(start_of(1 - core, sub), quarter)], mate_buf.at[index],
            pair_s.at[index], pair_r.at[index], {"col": col + 1 - 2 * core},
        )
        copy.start()
        pairs[index] = copy
    sends = {}

    def total(index, way, sub, far, store):
        pairs[index].wait_recv()
        block = ring_row(place + way * far, rows)
        terms = []
        for side in ((way,) if far else (1, -1)):
            if (side, sub, far + 1) in where:
                term = where[side, sub, far + 1]
                sends[term].wait_recv()
                terms.append(term)

        @pl.loop(0, quarter // strip)
        def _(step):
            at = pl.multiple_of(step * strip, strip)
            mine = pl.ds(pl.multiple_of(start_of(core, sub) + at, strip), strip)
            value = x_ref[block, mine, :].astype(jnp.float32)
            value = value + mate_buf[index, pl.ds(at, strip), :].astype(jnp.float32)
            for term in terms:
                value = value + got[term, pl.ds(at, strip), :].astype(jnp.float32)
            store(at, value)

    for index, way, sub, far in reversed(lanes):

        def keep(at, value, index=index):
            made[index, pl.ds(at, strip), :] = value.astype(jnp.bfloat16)

        total(index, way, sub, far, keep)
        copy = remote(
            made.at[index], got.at[index], ring_s.at[index], ring_r.at[index],
            {"row": ring_row(place + way, rows)},
        )
        copy.start()
        sends[index] = copy
    for index, way, sub, far in wanted[-2:]:

        def split(at, value, sub=sub):
            for piece in range(cols):
                last[piece, pl.ds(sub * quarter + at, strip), :] = value[
                    :, piece * part : (piece + 1) * part
                ].astype(jnp.bfloat16)

        total(index, way, sub, far, split)
    finals = []
    for step in range(1, cols):
        target = (col + step) % cols
        copy = remote(
            last.at[target], parts.at[col], col_s.at[step - 1], col_r.at[step - 1], {"col": target}
        )
        copy.start()
        finals.append(copy)
    parts[col] = last[col]
    for copy in finals:
        copy.wait()
    for half in range(2):
        value = parts[half].astype(jnp.float32)
        for other in range(half + 2, cols, 2):
            value = value + parts[other].astype(jnp.float32)
        out_ref[half * 2 * quarter : (half + 1) * 2 * quarter, :] = value
    for copy in pairs.values():
        copy.wait_send()
    for copy in sends.values():
        copy.wait_send()


def reduce(x):
    rows, cols = lax.axis_size("row"), lax.axis_size("col")
    tok, dim = x.shape[1:]
    count = len(lanes_of(rows))
    dma = pltpu.SemaphoreType.DMA
    vmem = lambda *shape: pltpu.VMEM(shape, jnp.bfloat16)
    return pl.pallas_call(
        functools.partial(reduce_kernel, rows, cols),
        out_shape=jax.ShapeDtypeStruct((tok, dim // cols), jnp.float32),
        in_specs=[pl.BlockSpec(memory_space=pltpu.VMEM)],
        out_specs=pl.BlockSpec(memory_space=pltpu.VMEM),
        scratch_shapes=[
            vmem(count + 2, tok // 4, dim), vmem(count, tok // 4, dim), vmem(count, tok // 4, dim),
            vmem(cols, tok // 2, dim // cols), vmem(cols, tok // 2, dim // cols),
            dma((count + 2,)), dma((count + 2,)), dma((count,)), dma((count,)),
            dma((cols - 1,)), dma((cols - 1,)),
        ],
        compiler_params=pltpu.CompilerParams(
            collective_id=1, has_side_effects=True, vmem_limit_bytes=60 * 1024 * 1024
        ),
        name="reduce",
    )(x)


def local(
    tokens, moe_gain, route_ids, route_weight, w_gate, w_up, w_down, next_gain, next_gate, next_ids
):
    rows = lax.axis_size("row")
    cols = lax.axis_size("col")
    tok, dim = tokens.shape
    experts = w_gate.shape[0]
    part = dim // cols
    col = lax.axis_index("col")
    row = lax.axis_index("row")
    floats = tokens.astype(jnp.float32)
    inverse = lax.rsqrt(jnp.mean(floats * floats, axis=-1, keepdims=True) + 1e-05)
    normed = (floats * inverse * moe_gain.astype(jnp.float32)).astype(jnp.bfloat16)
    gated_in = (floats * inverse * next_gain.astype(jnp.float32)).astype(jnp.bfloat16)

    info = jnp.concatenate([route_ids.astype(jnp.float32), route_weight], axis=1)
    everyone, info = gather(normed, info.T)
    info = jnp.swapaxes(info, 1, 2)
    mine = (row * experts + jnp.arange(experts, dtype=jnp.int32)).astype(jnp.float32)
    hit = info[:, :, :TOP, None] == mine
    mask = jnp.any(hit, axis=2)
    share = jnp.sum(jnp.where(hit, info[:, :, TOP:, None], 0.0), axis=2)
    lower = jnp.arange(tok)[None, :] < jnp.arange(tok)[:, None]
    place = jnp.einsum(
        "ut,stj->suj",
        lower.astype(jnp.bfloat16),
        mask.astype(jnp.bfloat16),
        preferred_element_type=jnp.float32,
    )
    place = jnp.where(mask, place, -1.0)
    pick = (
        jnp.swapaxes(place, 1, 2)[:, :, None, :]
        == jnp.arange(CAP, dtype=jnp.float32)[None, None, :, None]
    )
    weight = jnp.sum(jnp.where(pick, jnp.swapaxes(share, 1, 2)[:, :, None, :], 0.0), axis=3)
    onehot = pick.reshape(rows, experts * CAP, tok).astype(jnp.bfloat16)

    chosen = jnp.einsum("snt,std->snd", onehot, everyone, preferred_element_type=jnp.float32)
    chosen = chosen.astype(jnp.bfloat16).reshape(rows, experts, CAP, dim)
    chosen = jnp.swapaxes(chosen, 0, 1).reshape(experts, rows * CAP, dim)

    logits = jnp.dot(gated_in, next_gate, preferred_element_type=jnp.float32)
    width = next_gate.shape[1]
    index = next_ids - col * width
    owned = index[:, :, None] == jnp.arange(width, dtype=jnp.int32)[None, None, :]
    picked = jnp.sum(jnp.where(owned, logits[:, None, :], 0.0), axis=-1)
    high = jnp.max(logits, axis=-1, keepdims=True)
    total = jnp.sum(jnp.exp(logits - high), axis=-1, keepdims=True)
    stats = lax.all_gather(jnp.concatenate([high, total, picked], axis=1), "col")
    highest = jnp.max(stats[:, :, 0], axis=0)
    sums = jnp.sum(stats[:, :, 1] * jnp.exp(stats[:, :, 0] - highest), axis=0)
    next_logprob = (
        jnp.sum(stats[:, :, 2:], axis=0) - highest[:, None] - jnp.log(sums)[:, None]
    )

    gate = jnp.einsum("jmd,jdf->jmf", chosen, w_gate, preferred_element_type=jnp.float32)
    upward = jnp.einsum("jmd,jdf->jmf", chosen, w_up, preferred_element_type=jnp.float32)
    hidden = (jax.nn.silu(gate) * upward).astype(jnp.bfloat16)
    out = jnp.einsum("jmf,jfd->jmd", hidden, w_down, preferred_element_type=jnp.float32)
    scale = jnp.swapaxes(weight, 0, 1).reshape(experts, rows * CAP, 1)
    out = (out * scale).astype(jnp.bfloat16).reshape(experts, rows, CAP, dim)
    out = jnp.swapaxes(out, 0, 1).reshape(rows, experts * CAP, dim)
    mixed = jnp.einsum("snt,snd->std", onehot, out, preferred_element_type=jnp.float32)
    mixed = mixed.astype(jnp.bfloat16)
    mixed = reduce(mixed)
    residual = lax.dynamic_slice_in_dim(floats, col * part, part, 1)
    return ((residual + mixed).astype(jnp.bfloat16), next_logprob)


def solution(mesh):
    placed = (
        P("row", None),
        P(),
        P("row", None),
        P("row", None),
        P("row", None, "col"),
        P("row", None, "col"),
        P("row", "col", None),
        P(),
        P(None, "col"),
        P("row", None),
    )
    return jax.shard_map(
        local,
        mesh=mesh,
        in_specs=placed,
        out_specs=(P("row", "col"), P("row", None)),
        check_vma=False,
    )
```

time: 630 us -> 278 us (0.44); the launches traced: 619 us -> 277 us
  blocking collectives: 220 us -> 5.44 us
  local copies, waits for them, and re-layouts: 188 us -> 36.7 us
  Pallas kernels: 0 us -> 150 us
  waiting for transfers between devices: 105 us -> 0 us
  other arithmetic: 27.2 us -> 5.35 us
  matrix products: 57.4 us -> 78.8 us
  between operations: 14.4 us -> 0.83 us
    all_to_all x1 -> x0, blocking collectives: 205 us -> none  [local(): lax.all_to_all(buffer.reshape(row_count, local_experts, CAP, normed.shape...]
    pallas_call x0 -> x2, Pallas kernels: none -> 150 us  [the longest x1 79.6 us: reduce(): pl.pallas_call(functools.partial(reduce_kernel, rows, cols), out_shape=ja...]
    unnamed x21 -> x14, local copies, waits for them, and re-layouts: 132 us -> 3.7 us
    unnamed x2 -> x0, waiting for transfers between devices: 73.1 us -> none
    scatter x1 -> x0, local copies, waits for them, and re-layouts: 32.5 us -> none  [local(): buffer = buffer.at[target].set(normed[token_of])]
    all_to_all x1 -> x0, waiting for transfers between devices: 32 us -> none  [local(): lax.all_to_all(summed, 'row', split_axis=0, concat_axis=0, tiled=True)]
    dot_general x3 -> x6, matrix products: 55.3 us -> 78.1 us  [the longest x1 20.9 us: local(): jnp.einsum('jmd,jdf->jmf', chosen, w_up, preferred_element_type=jnp.float32)]
    another operation x3 -> x0, other arithmetic: 18.2 us -> none
  transfers between devices with their start and end apart: 2 -> 0, of which waited for: 2 -> 0; matrix products, arithmetic and copies ran while one was open for 1% -> 0% of each run, Pallas kernels for 0% -> 0%
where the time goes in v1:
time: 278 us; the launch traced here: 277 us
  Pallas kernels  150 us (54%)
  matrix products  78.8 us (28%)
  local copies, waits for them, and re-layouts  36.7 us (13%)
  blocking collectives  5.44 us (2%)
  other arithmetic  5.35 us (2%)
    pallas_call x1, Pallas kernels, reduce(): pl.pallas_call(functools.partial(reduce_kernel, rows, cols), out_shape=ja...  79.6 us
    pallas_call x1, Pallas kernels, gather(): pl.pallas_call(functools.partial(gather_kernel, rows, cols), out_shape=(j...  70.6 us
    dot_general x1, matrix products, local(): jnp.einsum('jmd,jdf->jmf', chosen, w_up, preferred_element_type=jnp.float32)  20.9 us
    dot_general x1, matrix products, local(): jnp.einsum('jmd,jdf->jmf', chosen, w_gate, preferred_element_type=jnp.flo...  18.9 us
    dot_general x1, matrix products, local(): jnp.einsum('jmf,jfd->jmd', hidden, w_down, preferred_element_type=jnp.flo...  18.2 us
    convert_element_type x1, local copies, waits for them, and re-layouts, local(): mixed = mixed.astype(jnp.bfloat16)  16.3 us
    dot_general x1, matrix products, local(): jnp.einsum('snt,std->snd', onehot, everyone, preferred_element_type=jnp.f...  10.4 us
    dot_general x1, matrix products, local(): jnp.einsum('snt,snd->std', onehot, out, preferred_element_type=jnp.float32)  9.46 us

profile of v1, /device:TPU:0, one launch (start us, length us, event | category | flops | bytes accessed | tf_op | source)
XLA Modules:
  0.0 277.3 jit_solution(14565977007659946163)
XLA Ops:
  0.6 0.0 copy-start
  0.6 0.0 copy-start.3
  0.7 0.0 copy-start.5
  0.7 1.9 copy.61
  2.5 0.4 multiply_reduce_fusion
  2.9 0.7 convert_element_type.44
  3.6 1.6 multiply_convert_fusion.3.x_ref
  5.3 0.0 copy-done.3
  5.3 0.0 copy-done.5
  5.3 0.6 maximum_bitcast_fusion.info_ref
  5.9 70.6 %gather.1 = (bf16[8,256,2880]{2,1,0:T(8,128)(2,1)}, f32[8,8,256]{2,1,0:T(8,128)}) custom-call(bf16[256,2880]{1,0:T(8,128)(2,1)} %multiply_convert_fusion.3.x_ref, f32[8,256]{1,0:T(8,128)} %maximum_bitcast_fusion.info_ref), custom_call_target="tpu_custom_call" | custom-call | tf_op jit(solution)/shard_map/gather/pallas_call | solution.py:125
  76.5 0.9 fusion.13
  77.4 0.1 compare_reduce_fusion
  77.5 0.2 convolution_select_fusion
  77.7 0.1 eq.56
  77.8 0.3 bitcast_compare_fusion
  78.1 10.4 %convolution_convert_fusion.1 = bf16[8,192,2880]{2,1,0:T(8,128)(2,1)} fusion(pred[8,192,256]{2,1,0:T(32,128)(4,1)S(1)} %bitcast_compare_fusion, bf16[8,256,2880]{2,1,0:T(8,128)(2,1)} %get-tuple-element.5), kind=kOutput, calls=%fused_computation.2 | convolution fusion | flops 2269347840 | bytes 21037056 | tf_op jit(solution)/shard_map/snt,std->snd/dot_general | solution.py:296
  88.6 7.8 %copy.63 = bf16[8,8,24,2880]{3,2,1,0:T(8,128)(2,1)} copy(bf16[8,8,24,2880]{3,2,0,1:T(8,128)(2,1)} %bitcast.56) | data formatting | bytes 17694720 | tf_op jit(solution)/shard_map/transpose | solution.py:298
  96.4 18.9 %fusion.15 = f32[8,192,720]{2,1,0:T(8,128)} fusion(bf16[8,192,2880]{2,1,0:T(8,128)(2,1)} %bitcast.57, bf16[8,2880,720]{1,2,0:T(8,128)(2,1)} %param.14), kind=kOutput, calls=%fused_computation.41 | convolution fusion | flops 6370099200 | bytes 46448640 | tf_op jit(solution)/shard_map/jmd,jdf->jmf/dot_general | solution.py:314
  115.3 20.9 %multiply_convert_fusion.8 = bf16[8,192,720]{2,1,0:T(8,128)(2,1)} fusion(f32[8,192,720]{2,1,0:T(8,128)} %fusion.15, bf16[8,192,2880]{2,1,0:T(8,128)(2,1)} %bitcast.58, bf16[8,2880,720]{1,2,0:T(8,128)(2,1)} %param.15), kind=kOutput, calls=%fused_computation.3.clone.clone.1 | convolution fusion | flops 6376734720 | bytes 48660480 | tf_op jit(solution)/shard_map/jmd,jdf->jmf/dot_general | solution.py:315
  136.2 0.1 fusion.6
  136.3 0.3 select_reduce_fusion
  136.6 0.1 mul.69
  136.7 18.2 %multiply_convert_fusion = bf16[8,192,2880]{2,1,0:T(8,128)(2,1)} fusion(f32[8,192]{1,0:T(8,128)S(1)} %mul.69, bf16[8,720,2880]{2,1,0:T(8,128)(2,1)} %param.16, bf16[8,192,720]{2,1,0:T(8,128)(2,1)} %multiply_convert_fusion.8), kind=kOutput, calls=%fused_computation | convolution fusion | flops 6378946560 | bytes 44242944 | tf_op jit(solution)/shard_map/jmf,jfd->jmd/dot_general | solution.py:317
  154.9 7.8 %copy.65 = bf16[8,8,24,2880]{3,2,1,0:T(8,128)(2,1)} copy(bf16[8,8,24,2880]{3,2,0,1:T(8,128)(2,1)} %bitcast.59) | data formatting | bytes 17694720 | tf_op jit(solution)/shard_map/transpose | solution.py:320
  162.8 9.5 %convolution_convert_fusion = bf16[8,256,2880]{1,2,0:T(8,128)(2,1)} fusion(pred[8,192,256]{2,1,0:T(32,128)(4,1)S(1)} %bitcast_compare_fusion, bf16[8,192,2880]{2,1,0:T(8,128)(2,1)} %bitcast.55), kind=kOutput, calls=%fused_computation.1 | convolution fusion | flops 2270822400 | bytes 21037056 | tf_op jit(solution)/shard_map/snt,snd->std/dot_general | solution.py:321
  172.2 16.3 %copy.66.x_ref = bf16[8,256,2880]{2,1,0:T(8,128)(2,1)} copy(bf16[8,256,2880]{1,2,0:T(8,128)(2,1)} %convolution_convert_fusion) | data formatting | bytes 23592960 | tf_op jit(solution)/shard_map/convert_element_type | solution.py:322
  188.5 79.6 %reduce.2 = f32[256,720]{1,0:T(8,128)} custom-call(bf16[8,256,2880]{2,1,0:T(8,128)(2,1)} %copy.66.x_ref), custom_call_target="tpu_custom_call" | custom-call | tf_op jit(solution)/shard_map/reduce/pallas_call | solution.py:241
  268.0 0.0 copy-start.1
  268.1 0.0 copy-start.2
  268.1 0.0 copy-start.4
  268.1 0.2 convert_element_type.43
  268.3 0.9 copy-done.1
  269.2 0.3 add_convert_fusion
  269.5 0.9 copy.67
  270.4 0.0 copy-done.2
  270.4 0.0 copy-done
  270.4 0.7 fusion.14
  271.1 0.0 copy-done.4
  271.2 5.4 %all-gather = f32[1024,6]{0,1:T(8,128)S(1)} all-gather(f32[256,6]{0,1:T(8,128)S(1)} %pad_maximum_fusion), channel_id=2, replica_groups=mesh['col'=4,'row'=8] {'col'}, dimensions={0}, use_global_device_ids=true | all-gather | bytes 30720 | tf_op jit(solution)/shard_map/all_gather | solution.py:307
  276.7 0.6 subtract_subtract_fusion
  (15 shorter events, 0.2 us)
Async XLA Ops:
  0.6 269.8 %copy-start = (bf16[2880,32]{0,1:T(8,128)(2,1)S(1)}, bf16[2880,32]{0,1:T(8,128)(2,1)}, u32[]{:S(2)}) copy-start(bf16[2880,32]{0,1:T(8,128)(2,1)} %param.18) | copy-start | bytes 552964
  0.6 4.6 %copy-start.3 = (s32[256,4]{0,1:T(4,128)S(1)}, s32[256,4]{0,1:T(4,128)}, u32[]{:S(2)}) copy-start(s32[256,4]{0,1:T(4,128)} %param.12) | copy-start | bytes 12292
  0.7 4.6 %copy-start.5 = (f32[256,4]{0,1:T(4,128)S(1)}, f32[256,4]{0,1:T(4,128)}, u32[]{:S(2)}) copy-start(f32[256,4]{0,1:T(4,128)} %param.13) | copy-start | bytes 12292
  268.0 1.1 copy-start.1
  268.1 2.3 copy-start.2
  268.1 3.0 %copy-start.4 = (s32[256,4]{0,1:T(4,128)S(1)}, s32[256,4]{0,1:T(4,128)}, u32[]{:S(2)}) copy-start(s32[256,4]{0,1:T(4,128)} %param.19) | copy-start | bytes 12292

commit v2 on v1

--- a/solution.py
+++ b/solution.py
@@ -256,6 +256,57 @@
     )(x)
 
 
+def place_kernel(pick_ref, x_ref, out_ref):
+    value = jnp.dot(pick_ref[0], x_ref[0], preferred_element_type=jnp.float32)
+    experts, _, slots, _ = out_ref.shape
+    for expert in range(experts):
+        out_ref[expert, 0] = value[expert * slots : (expert + 1) * slots].astype(jnp.bfloat16)
+
+
+def place_tokens(pick, x, experts):
+    rows, count, tok = pick.shape
+    dim = x.shape[2]
+    slots = count // experts
+    return pl.pallas_call(
+        place_kernel,
+        grid=(rows,),
+        out_shape=jax.ShapeDtypeStruct((experts, rows, slots, dim), jnp.bfloat16),
+        in_specs=[
+            pl.BlockSpec((1, count, tok), lambda s: (s, 0, 0)),
+            pl.BlockSpec((1, tok, dim), lambda s: (s, 0, 0)),
+        ],
+        out_specs=pl.BlockSpec((experts, 1, slots, dim), lambda s: (0, s, 0, 0)),
+        name="place",
+    )(pick, x)
+
+
+def join_kernel(back_ref, x_ref, out_ref, flat):
+    experts, _, slots, _ = x_ref.shape
+    for expert in range(experts):
+        flat[expert * slots : (expert + 1) * slots, :] = x_ref[expert, 0].astype(jnp.float32)
+    value = jnp.dot(
+        back_ref[0], flat[...].astype(jnp.bfloat16), preferred_element_type=jnp.float32
+    )
+    out_ref[0] = value.astype(jnp.bfloat16)
+
+
+def join_tokens(back, x):
+    rows, tok, count = back.shape
+    experts, _, slots, dim = x.shape
+    return pl.pallas_call(
+        join_kernel,
+        grid=(rows,),
+        out_shape=jax.ShapeDtypeStruct((rows, tok, dim), jnp.bfloat16),
+        in_specs=[
+            pl.BlockSpec((1, tok, count), lambda s: (s, 0, 0)),
+            pl.BlockSpec((experts, 1, slots, dim), lambda s: (0, s, 0, 0)),
+        ],
+        out_specs=pl.BlockSpec((1, tok, dim), lambda s: (s, 0, 0)),
+        scratch_shapes=[pltpu.VMEM((count, dim), jnp.float32)],
+        name="join",
+    )(back, x)
+
+
 def local(
     tokens, moe_gain, route_ids, route_weight, w_gate, w_up, w_down, next_gain, next_gate, next_ids
 ):
@@ -293,9 +344,7 @@
     weight = jnp.sum(jnp.where(pick, jnp.swapaxes(share, 1, 2)[:, :, None, :], 0.0), axis=3)
     onehot = pick.reshape(rows, experts * CAP, tok).astype(jnp.bfloat16)
 
-    chosen = jnp.einsum("snt,std->snd", onehot, everyone, preferred_element_type=jnp.float32)
-    chosen = chosen.astype(jnp.bfloat16).reshape(rows, experts, CAP, dim)
-    chosen = jnp.swapaxes(chosen, 0, 1).reshape(experts, rows * CAP, dim)
+    chosen = place_tokens(onehot, everyone, experts).reshape(experts, rows * CAP, dim)
 
     logits = jnp.dot(gated_in, next_gate, preferred_element_type=jnp.float32)
     width = next_gate.shape[1]
@@ -317,9 +366,7 @@
     out = jnp.einsum("jmf,jfd->jmd", hidden, w_down, preferred_element_type=jnp.float32)
     scale = jnp.swapaxes(weight, 0, 1).reshape(experts, rows * CAP, 1)
     out = (out * scale).astype(jnp.bfloat16).reshape(experts, rows, CAP, dim)
-    out = jnp.swapaxes(out, 0, 1).reshape(rows, experts * CAP, dim)
-    mixed = jnp.einsum("snt,snd->std", onehot, out, preferred_element_type=jnp.float32)
-    mixed = mixed.astype(jnp.bfloat16)
+    mixed = join_tokens(jnp.swapaxes(onehot, 1, 2), out)
     mixed = reduce(mixed)
     residual = lax.dynamic_slice_in_dim(floats, col * part, part, 1)
     return ((residual + mixed).astype(jnp.bfloat16), next_logprob)

time: 278 us -> 259 us (0.932)
  local copies, waits for them, and re-layouts: 36.7 us -> 7.21 us
  Pallas kernels: 150 us -> 174 us
  matrix products: 78.8 us -> 58.5 us
  other arithmetic: 5.35 us -> 12.5 us
    pallas_call x0 -> x2, Pallas kernels: none -> 23.9 us  [the longest x1 12.3 us: join_tokens(): pl.pallas_call(join_kernel, grid=(rows,), out_shape=jax.ShapeDtypeStruct(...]
    dot_general x2 -> x0, matrix products: 19.9 us -> none  [the longest x1 10.4 us: local(): jnp.einsum('snt,std->snd', onehot, everyone, preferred_element_type=jnp.f...]
    transpose x2 -> x0, local copies, waits for them, and re-layouts: 15.6 us -> none  [the longest x1 7.83 us: local(): out = jnp.swapaxes(out, 0, 1).reshape(rows, experts * CAP, dim)]
    convert_element_type x1, local copies, waits for them, and re-layouts: 16.3 us -> 1.26 us  [local(): onehot = pick.reshape(rows, experts * CAP, tok).astype(jnp.bfloat16)]
    transpose x0 -> x1, other arithmetic: none -> 2.79 us  [local(): mixed = join_tokens(jnp.swapaxes(onehot, 1, 2), out)]
where the time goes in v2:
time: 259 us; the launch traced here: 258 us
  Pallas kernels  174 us (67%)
  matrix products  58.5 us (23%)
  other arithmetic  12.5 us (5%)
  local copies, waits for them, and re-layouts  7.21 us (3%)
  blocking collectives  5.44 us (2%)
    pallas_call x1, Pallas kernels, reduce(): pl.pallas_call(functools.partial(reduce_kernel, rows, cols), out_shape=ja...  79.5 us
    pallas_call x1, Pallas kernels, gather(): pl.pallas_call(functools.partial(gather_kernel, rows, cols), out_shape=(j...  70.6 us
    dot_general x1, matrix products, local(): jnp.einsum('jmd,jdf->jmf', chosen, w_up, preferred_element_type=jnp.float32)  20.9 us
    dot_general x1, matrix products, local(): jnp.einsum('jmd,jdf->jmf', chosen, w_gate, preferred_element_type=jnp.flo...  18.8 us
    dot_general x1, matrix products, local(): jnp.einsum('jmf,jfd->jmd', hidden, w_down, preferred_element_type=jnp.flo...  17.9 us
    pallas_call x1, Pallas kernels, join_tokens(): pl.pallas_call(join_kernel, grid=(rows,), out_shape=jax.ShapeDtypeStruct(...  12.3 us
    pallas_call x1, Pallas kernels, place_tokens(): pl.pallas_call(place_kernel, grid=(rows,), out_shape=jax.ShapeDtypeStruct...  11.7 us
    all_gather x1, blocking collectives, local(): lax.all_gather(jnp.concatenate([high, total, picked], axis=1), 'col')  5.44 us

profile of v2, /device:TPU:0, one launch (start us, length us, event | category | flops | bytes accessed | tf_op | source)
XLA Modules:
  0.0 258.5 jit_solution(3452015077356170445)
XLA Ops:
  0.6 0.0 copy-start
  0.6 1.9 copy.51
  2.5 0.0 copy-start.3
  2.5 0.0 copy-start.5
  2.5 0.7 convert_element_type.40
  3.2 0.4 multiply_reduce_fusion
  3.6 1.7 multiply_convert_fusion.3.x_ref
  5.3 0.0 copy-done.3
  5.3 0.0 copy-done.5
  5.3 0.6 maximum_bitcast_fusion.info_ref
  5.9 70.6 %gather.1 = (bf16[8,256,2880]{2,1,0:T(8,128)(2,1)}, f32[8,8,256]{2,1,0:T(8,128)}) custom-call(bf16[256,2880]{1,0:T(8,128)(2,1)} %multiply_convert_fusion.3.x_ref, f32[8,256]{1,0:T(8,128)} %maximum_bitcast_fusion.info_ref), custom_call_target="tpu_custom_call" | custom-call | tf_op jit(solution)/shard_map/gather/pallas_call | solution.py:125
  76.5 0.9 fusion.13
  77.4 0.1 compare_reduce_fusion
  77.6 0.2 convolution_select_fusion
  77.7 0.2 eq.53
  77.9 1.9 copy.52
  79.8 0.1 eq.56
  79.8 2.8 %fusion.23.back_ref = bf16[8,256,192]{2,1,0:T(8,128)(2,1)} fusion(f32[8,192,256]{1,2,0:T(8,128)} %copy.52, f32[192]{0:T(256)S(1)} %eq.56), kind=kLoop, calls=%fused_computation.40 | loop fusion | flops 786432 | bytes 2360064 | tf_op jit(solution)/shard_map/transpose | solution.py:369
  82.6 0.1 fusion.6
  82.7 0.3 select_reduce_fusion
  83.0 0.1 mul.69
  83.1 1.8 compare_convert_fusion
  84.9 1.3 copy.54.pick_ref
  86.2 11.7 %place.1 = bf16[8,8,24,2880]{3,2,1,0:T(8,128)(2,1)} custom-call(bf16[8,192,256]{2,1,0:T(8,128)(2,1)} %copy.54.pick_ref, bf16[8,256,2880]{2,1,0:T(8,128)(2,1)} %get-tuple-element.5.x_ref), custom_call_target="tpu_custom_call" | custom-call | tf_op jit(solution)/shard_map/place/pallas_call | solution.py:270
  97.9 18.8 %fusion.15 = f32[8,192,720]{2,1,0:T(8,128)} fusion(bf16[8,192,2880]{2,1,0:T(8,128)(2,1)} %bitcast.46, bf16[8,2880,720]{1,2,0:T(8,128)(2,1)} %param.14), kind=kOutput, calls=%fused_computation.39 | convolution fusion | flops 6370099200 | bytes 46448640 | tf_op jit(solution)/shard_map/jmd,jdf->jmf/dot_general | solution.py:363
  116.7 20.9 %multiply_convert_fusion.8 = bf16[8,192,720]{2,1,0:T(8,128)(2,1)} fusion(f32[8,192,720]{2,1,0:T(8,128)} %fusion.15, bf16[8,192,2880]{2,1,0:T(8,128)(2,1)} %bitcast.47, bf16[8,2880,720]{1,2,0:T(8,128)(2,1)} %param.15), kind=kOutput, calls=%fused_computation.1.clone.clone.1 | convolution fusion | flops 6376734720 | bytes 48660480 | tf_op jit(solution)/shard_map/jmd,jdf->jmf/dot_general | solution.py:364
  137.6 17.9 %multiply_convert_fusion = bf16[8,192,2880]{2,1,0:T(8,128)(2,1)} fusion(f32[8,192]{1,0:T(8,128)S(1)} %mul.69, bf16[8,720,2880]{2,1,0:T(8,128)(2,1)} %param.16, bf16[8,192,720]{2,1,0:T(8,128)(2,1)} %multiply_convert_fusion.8), kind=kOutput, calls=%fused_computation | convolution fusion | flops 6378946560 | bytes 44242944 | tf_op jit(solution)/shard_map/jmf,jfd->jmd/dot_general | solution.py:366
  155.5 12.3 %join.1.x_ref = bf16[8,256,2880]{2,1,0:T(8,128)(2,1)} custom-call(bf16[8,256,192]{2,1,0:T(8,128)(2,1)} %fusion.23.back_ref, bf16[8,8,24,2880]{3,2,1,0:T(8,128)(2,1)} %bitcast.48), custom_call_target="tpu_custom_call" | custom-call | tf_op jit(solution)/shard_map/join/pallas_call | solution.py:296
  167.8 79.5 %reduce.2 = f32[256,720]{1,0:T(8,128)} custom-call(bf16[8,256,2880]{2,1,0:T(8,128)(2,1)} %join.1.x_ref), custom_call_target="tpu_custom_call" | custom-call | tf_op jit(solution)/shard_map/reduce/pallas_call | solution.py:241
  247.3 0.0 copy-start.1
  247.3 0.0 copy-start.2
  247.3 1.8 convert_element_type.39
  249.1 0.0 copy-start.4
  249.1 0.0 copy-done.1
  249.1 1.5 add_convert_fusion
  250.6 0.9 copy.56
  251.5 0.0 copy-done.2
  251.5 0.0 copy-done
  251.5 0.7 fusion.14
  252.2 0.0 copy-done.4
  252.3 5.4 %all-gather = f32[1024,6]{0,1:T(8,128)S(1)} all-gather(f32[256,6]{0,1:T(8,128)S(1)} %pad_maximum_fusion), channel_id=2, replica_groups=mesh['col'=4,'row'=8] {'col'}, dimensions={0}, use_global_device_ids=true | all-gather | bytes 30720 | tf_op jit(solution)/shard_map/all_gather | solution.py:356
  257.9 0.6 subtract_subtract_fusion
  (15 shorter events, 0.2 us)
Async XLA Ops:
  0.6 250.9 %copy-start = (bf16[2880,32]{0,1:T(8,128)(2,1)S(1)}, bf16[2880,32]{0,1:T(8,128)(2,1)}, u32[]{:S(2)}) copy-start(bf16[2880,32]{0,1:T(8,128)(2,1)} %param.18) | copy-start | bytes 552964
  2.5 2.8 %copy-start.3 = (s32[256,4]{0,1:T(4,128)S(1)}, s32[256,4]{0,1:T(4,128)}, u32[]{:S(2)}) copy-start(s32[256,4]{0,1:T(4,128)} %param.12) | copy-start | bytes 12292
  2.5 2.8 %copy-start.5 = (f32[256,4]{0,1:T(4,128)S(1)}, f32[256,4]{0,1:T(4,128)}, u32[]{:S(2)}) copy-start(f32[256,4]{0,1:T(4,128)} %param.13) | copy-start | bytes 12292
  247.3 1.8 copy-start.1
  247.3 4.2 %copy-start.2 = (bf16[2880]{0:T(1024)(128)(2,1)S(1)}, bf16[2880]{0:T(1024)(128)(2,1)}, u32[]{:S(2)}) copy-start(bf16[2880]{0:T(1024)(128)(2,1)} %param.17) | copy-start | bytes 17284
  249.1 3.1 %copy-start.4 = (s32[256,4]{0,1:T(4,128)S(1)}, s32[256,4]{0,1:T(4,128)}, u32[]{:S(2)}) copy-start(s32[256,4]{0,1:T(4,128)} %param.19) | copy-start | bytes 12292
